TPU v7x, 32 devices: a whole 2x2x4 slice. The times are simulated.
32 devices in a mesh: pole: 2 (over y), row: 4 (over z), col: 4 (over x, core).
Axes of the slice: x: 2, y: 2, z: 4, core: 2. Of those that a mesh axis runs over, the one named last changes fastest.
Arguments:
- ainv_cc: bfloat16 [2048, 1024], P(('pole', 'row'), 'col'), parts along dimension 0, may hold values from -6 to 6
- factor: bfloat16 [4, 1024, 1024], P('pole', 'row', 'col'), parts along dimension 0, may hold values from -0.375 to 0.375
- inv_pivot: float32 [4, 1024, 1024], P('pole', 'row', 'col'), parts along dimension 0, may hold values from -6 to 6
- pattern: int32 [2, 8], replicated, may hold values from 0 to 1, as said below
Outputs:
- ainv_kc: bfloat16 [4, 1024, 1024], P('pole', 'col', 'row'), parts along dimension 0
- ainv_kk: float32 [4, 1024, 1024], P('pole', 'row', 'col'), parts along dimension 0
There are 2 independent parts, one for each index of `pole`. A program takes and returns all parts, laid end to end along the dimension named above; an argument that names none is the same for every part. Nothing has to cross between parts.
Inputs may be any that keep to these rules, and one draw needn't show every extreme that they name: `pattern`: for each supernode, each aligned group of 2 consecutive blocks (blocks g * 2 to (g + 1) * 2 - 1) holds at most 1 nonzero blocks, and some group holds exactly 1.
All inputs are finite; a program needn't handle non-finite values.
Results may differ from a plain program's by a relative error of at most 0.012.
Values may be sent and summed in bfloat16 or wider, within the bound.
A program may use at most 64 MiB of HBM per device.

v0:
```python
import jax
import jax.numpy as jnp
from jax import lax
from jax.sharding import PartitionSpec as P

BLK = 128
SUPERS = 2
RB_DEV = 2


def spread(x, axis, root):
    mine = lax.axis_index(axis) == root
    return lax.psum(jnp.where(mine, x, jnp.zeros_like(x)), axis)


def body(ainv_cc, factor, inv_pivot, pattern):
    rows_here = factor.shape[1]
    width_part = factor.shape[2]
    per_col = lax.axis_size("row") // lax.axis_size("col")
    row_index = lax.axis_index("row")
    col_index = lax.axis_index("col")
    full_width = lax.all_gather(factor, "col", axis=2, tiled=True)
    full_cols = full_width.shape[2]
    own_marks = lax.dynamic_slice_in_dim(pattern, row_index * RB_DEV, RB_DEV, 1)
    blocks = full_width.reshape(SUPERS, RB_DEV, BLK, full_cols)
    masked = jnp.where(own_marks[:, :, None, None] > 0, blocks, jnp.zeros_like(blocks))
    local_factor = masked.reshape(SUPERS, rows_here, full_cols)
    received = []
    for section in range(per_col):
        received.append(spread(local_factor, "row", col_index * per_col + section))
    gathered_rows = jnp.concatenate(received, axis=1)
    left_list = [ainv_cc for super_index in range(SUPERS)]
    cross_list = []
    diag_list = []
    for super_index in range(SUPERS):
        rows_matrix = gathered_rows[super_index]
        operand = left_list[super_index]
        factor_rows = local_factor[super_index]

        def column_term(first_row, row_count, rows_matrix=rows_matrix, operand=operand):
            return lax.dot_general(
                rows_matrix, operand, (((0,), (1,)), ((), ())), preferred_element_type=jnp.float32
            )

        summed = lax.psum_scatter(
            column_term(jnp.int32(0), lax.axis_size("col") * width_part).astype(jnp.bfloat16),
            "col",
            scatter_dimension=0,
            tiled=True,
        ).astype(jnp.float32)
        cross_block = (-summed).astype(jnp.bfloat16)

        def diagonal_term(first_row, row_count, factor_rows=factor_rows, cross_block=cross_block):
            return lax.dot_general(
                factor_rows,
                cross_block,
                (((0,), (1,)), ((), ())),
                preferred_element_type=jnp.float32,
            )

        update = lax.psum_scatter(
            diagonal_term(
                jnp.int32(0), lax.axis_size("row") * (full_cols // lax.axis_size("row"))
            ).astype(jnp.bfloat16),
            "row",
            scatter_dimension=0,
            tiled=True,
        ).astype(jnp.float32)
        cross_list.append(cross_block)
        diag_list.append(inv_pivot[super_index] - update)
    return (jnp.stack(cross_list), jnp.stack(diag_list))


def solution(mesh):
    placed = (P(("pole", "row"), "col"), P("pole", "row", "col"), P("pole", "row", "col"), P())
    return jax.shard_map(
        body,
        mesh=mesh,
        in_specs=placed,
        out_specs=(P("pole", "col", "row"), P("pole", "row", "col")),
        check_vma=False,
    )
```

profile of v0, /device:TPU:1, one launch (start us, length us, event | category | flops | bytes accessed | tf_op | source)
XLA Modules:
  0.0 184.7 jit_solution(14719530490384037543)
XLA Ops:
  7.2 0.0 copy-start
  7.2 0.0 all-gather.2.cloned.1.call-start
  7.2 0.7 all-gather.2.cloned.1.call-update
  7.9 0.0 all-reduce.2.cloned.1.call-start
  8.0 0.0 copy-start.6
  8.0 0.7 copy-done.6
  8.6 0.1 dynamic-slice_compare_fusion
  8.7 0.1 broadcast_bitcast_fusion
  8.8 20.1 %all-gather.2.cloned.1.call-done = bf16[2,256,1024]{2,1,0:T(8,128)(2,1)} async-done(((bf16[2,256,256]{2,1,0:T(8,128)(2,1)}), bf16[2,256,1024]{2,1,0:T(8,128)(2,1)}) %all-gather.2.cloned.1.call-update) | async-done | bytes 1048592 | tf_op jit(solution)/shard_map/all_gather | solution.py:22
  28.9 2.4 %select_select_fusion = bf16[2,256,1024]{2,1,0:T(8,128)(2,1)} fusion(bf16[2,256,1024]{2,1,0:T(8,128)(2,1)} %all-gather.2.cloned.1.call-done, pred[2,256]{1,0:T(4,128)(4,1)S(1)} %bitcast.37, pred[]{:T(512)S(6)} %eq.3), kind=kLoop, calls=%fused_computation.4 | loop fusion | flops 1048576 | bytes 2097665 | tf_op jit(solution)/shard_map/jit(_where)/select_n | solution.py:13
  31.3 0.0 all-reduce.2.cloned.1.call-update
  31.3 0.0 reduce-scatter.7.cloned.1.call-start
  31.4 51.7 %all-reduce.2.cloned.1.call-done = bf16[2,256,1024]{2,1,0:T(8,128)(2,1)} async-done(((bf16[2,256,1024]{2,1,0:T(8,128)(2,1)}), bf16[2,256,1024]{2,1,0:T(8,128)(2,1)}) %all-reduce.2.cloned.1.call-update) | async-done | bytes 1048592 | tf_op jit(solution)/shard_map/psum | solution.py:13
  83.1 0.0 copy-done
  83.1 0.0 copy-start.2
  83.1 2.3 %convolution_convert_fusion.2 = bf16[1024,256]{1,0:T(8,128)(2,1)} fusion(bf16[256,256]{1,0:T(8,128)(2,1)S(1)} %copy-done, bf16[2,256,1024]{2,1,0:T(8,128)(2,1)} %all-reduce.2.cloned.1.call-done), kind=kOutput, calls=%fused_computation.2 | convolution fusion | flops 134479872 | bytes 1179648 | tf_op jit(solution)/shard_map/dot_general | solution.py:41
  85.4 0.0 copy-start.1
  85.4 0.0 reduce-scatter.7.cloned.1.call-update
  85.4 0.0 reduce-scatter.5.cloned.1.call-start
  85.5 0.0 copy-done.2
  85.5 1.2 convolution_convert_fusion.3
  86.7 0.0 reduce-scatter.5.cloned.1.call-update
  86.7 0.0 reduce-scatter.11.cloned.1.call-start
  86.7 0.0 copy-done.1
  86.7 0.1 broadcast_select_fusion
  86.9 0.1 fusion.4
  87.0 20.2 %reduce-scatter.7.cloned.1.call-done = bf16[256,256]{1,0:T(8,128)(2,1)} async-done(((bf16[1024,256]{1,0:T(8,128)(2,1)}), bf16[256,256]{1,0:T(8,128)(2,1)}) %reduce-scatter.7.cloned.1.call-update) | async-done | bytes 131088 | tf_op jit(solution)/shard_map/reduce_scatter | solution.py:45
  107.2 2.1 %convolution_convert_fusion = bf16[1024,256]{1,0:T(8,128)(2,1)} fusion(bf16[256,1024]{1,0:T(8,128)(2,1)S(1)} %bitcast.36, bf16[256,256]{1,0:T(8,128)(2,1)} %reduce-scatter.7.cloned.1.call-done), kind=kOutput, calls=%fused_computation | convolution fusion | flops 134676480 | bytes 1179648 | tf_op jit(solution)/shard_map/dot_general | solution.py:54
  109.2 0.0 reduce-scatter.11.cloned.1.call-update
  109.3 0.0 reduce-scatter.9.cloned.1.call-start
  109.3 21.9 %reduce-scatter.5.cloned.1.call-done = bf16[256,256]{1,0:T(8,128)(2,1)} async-done(((bf16[1024,256]{1,0:T(8,128)(2,1)}), bf16[256,256]{1,0:T(8,128)(2,1)}) %reduce-scatter.5.cloned.1.call-update) | async-done | bytes 131088 | tf_op jit(solution)/shard_map/reduce_scatter | solution.py:45
  131.2 2.1 %convolution_convert_fusion.1 = bf16[1024,256]{1,0:T(8,128)(2,1)} fusion(bf16[256,1024]{1,0:T(8,128)(2,1)S(1)} %bitcast.35, bf16[256,256]{1,0:T(8,128)(2,1)} %reduce-scatter.5.cloned.1.call-done), kind=kOutput, calls=%fused_computation.1 | convolution fusion | flops 134676480 | bytes 1179648 | tf_op jit(solution)/shard_map/dot_general | solution.py:54
  133.3 0.0 copy-start.3
  133.3 0.0 reduce-scatter.9.cloned.1.call-update
  133.3 0.9 copy-done.3
  134.2 0.0 copy-start.4
  134.2 0.0 copy-start.5
  134.2 0.9 copy-done.4
  135.1 0.7 pad_maximum_fusion.1
  135.8 17.6 %reduce-scatter.11.cloned.1.call-done = bf16[256,256]{1,0:T(8,128)(2,1)} async-done(((bf16[1024,256]{1,0:T(8,128)(2,1)}), bf16[256,256]{1,0:T(8,128)(2,1)}) %reduce-scatter.11.cloned.1.call-update) | async-done | bytes 131088 | tf_op jit(solution)/shard_map/reduce_scatter | solution.py:61
  153.4 22.5 %reduce-scatter.9.cloned.1.call-done = bf16[256,256]{1,0:T(8,128)(2,1)} async-done(((bf16[1024,256]{1,0:T(8,128)(2,1)}), bf16[256,256]{1,0:T(8,128)(2,1)}) %reduce-scatter.9.cloned.1.call-update) | async-done | bytes 131088 | tf_op jit(solution)/shard_map/reduce_scatter | solution.py:61
  176.0 0.0 copy-done.5
  176.0 1.0 fusion.1
  177.0 0.8 pad_maximum_fusion
  (3 shorter events, 0.1 us)
Async XLA Ops:
  7.2 76.0 %copy-start = (bf16[256,256]{1,0:T(8,128)(2,1)S(1)}, bf16[256,256]{1,0:T(8,128)(2,1)}, u32[]{:S(2)}) copy-start(bf16[256,256]{1,0:T(8,128)(2,1)} %param.4) | copy-start | bytes 393220
  7.2 21.8 %all-gather.2.cloned.1.call-start = ((), (), s32[]{:S(2)}) async-start(), calls=%async_computation.4 | async-start | bytes 1310720 | tf_op jit(solution)/shard_map/all_gather | solution.py:22
  7.9 75.2 %all-reduce.2.cloned.1.call-start = ((), (), s32[]{:S(2)}) async-start(), calls=%async_computation.5 | async-start | bytes 2097152 | tf_op jit(solution)/shard_map/psum | solution.py:13
  8.0 0.7 copy-start.6
  31.3 75.9 %reduce-scatter.7.cloned.1.call-start = ((), (), s32[]{:S(2)}) async-start(), calls=%async_computation.7 | async-start | bytes 655360 | tf_op jit(solution)/shard_map/reduce_scatter | solution.py:45
  83.1 2.4 %copy-start.2 = (bf16[2,256,1024]{2,1,0:T(8,128)(2,1)S(1)}, bf16[2,256,1024]{2,1,0:T(8,128)(2,1)}, u32[]{:S(2)}) copy-start(bf16[2,256,1024]{2,1,0:T(8,128)(2,1)} %all-reduce.2.cloned.1.call-done) | copy-start | bytes 3145732
  85.4 1.3 copy-start.1
  85.4 45.8 %reduce-scatter.5.cloned.1.call-start = ((), (), s32[]{:S(2)}) async-start(), calls=%async_computation.6 | async-start | bytes 655360 | tf_op jit(solution)/shard_map/reduce_scatter | solution.py:45
  86.7 66.8 %reduce-scatter.11.cloned.1.call-start = ((), (), s32[]{:S(2)}) async-start(), calls=%async_computation.9 | async-start | bytes 655360 | tf_op jit(solution)/shard_map/reduce_scatter | solution.py:61
  109.3 66.7 %reduce-scatter.9.cloned.1.call-start = ((), (), s32[]{:S(2)}) async-start(), calls=%async_computation.8 | async-start | bytes 655360 | tf_op jit(solution)/shard_map/reduce_scatter | solution.py:61
  133.3 0.9 copy-start.3
  134.2 0.9 copy-start.4
  134.2 41.8 %copy-start.5 = (f32[2,256,256]{2,1,0:T(8,128)S(1)}, f32[2,256,256]{2,1,0:T(8,128)}, u32[]{:S(2)}) copy-start(f32[2,256,256]{2,1,0:T(8,128)} %param.6) | copy-start | bytes 1572868
Sparse Core Ops, SparseCore 0:
  9.6 19.3 all-gather.1
  31.4 51.6 all-reduce.1
  86.3 20.7 reduce-scatter.6
  109.5 21.6 reduce-scatter.4
  133.4 19.9 reduce-scatter.10
  156.2 19.6 reduce-scatter.8
where the time goes:
time: 188 us; the launch traced here: 185 us
  waiting for transfers between devices  155 us (82%)
  between operations  14.2 us (8%)
  matrix products  7.57 us (4%)
  other arithmetic  5.21 us (3%)
  local copies, waits for them, and re-layouts  2.6 us (1%)
    psum x1, waiting for transfers between devices, spread(): return lax.psum(jnp.where(mine, x, jnp.zeros_like(x)), axis)  51.7 us
    reduce_scatter x2, waiting for transfers between devices, body(): lax.psum_scatter(column_term(jnp.int32(0), lax.axis_size('col') * width_p...  42.1 us
    reduce_scatter x2, waiting for transfers between devices, body(): lax.psum_scatter(diagonal_term(jnp.int32(0), lax.axis_size('row') * (full...  40.1 us
    all_gather x1, waiting for transfers between devices, body(): full_width = lax.all_gather(factor, 'col', axis=2, tiled=True)  20.1 us
    dot_general x2, matrix products, diagonal_term(): lax.dot_general(factor_rows, cross_block, (((0,), (1,)), ((), ())), prefe...  4.12 us
  transfers between devices with their start and end apart: 6, of which 6 were waited for; matrix products, arithmetic and copies ran while one was open for 3% of the time, Pallas kernels for 0%

commit v1 on v0

--- a/solution.py
+++ b/solution.py
@@ -1,6 +1,10 @@
+import functools
+
 import jax
 import jax.numpy as jnp
 from jax import lax
+from jax.experimental import pallas as pl
+from jax.experimental.pallas import tpu as pltpu
 from jax.sharding import PartitionSpec as P
 
 BLK = 128
@@ -71,10 +75,328 @@
     return (jnp.stack(cross_list), jnp.stack(diag_list))
 
 
+def remote(src, dst, send_sem, recv_sem, row, col):
+    return pltpu.make_async_remote_copy(
+        src_ref=src,
+        dst_ref=dst,
+        send_sem=send_sem,
+        recv_sem=recv_sem,
+        device_id={"row": row, "col": col},
+        device_id_type=pl.DeviceIdType.MESH,
+    )
+
+
+def kernel(
+    n, pat, f_ref, a_ref, p_ref, kc_ref, kk_ref,
+    mc, mr, af, ac, y,
+    zm_send, zm_recv, za_send, za_recv, pa_send, pa_recv, pc_send, pc_recv, pm_send, pm_recv,
+):
+    r = lax.axis_index("row")
+    c = lax.axis_index("col")
+    sib = c + 1 - 2 * lax.rem(c, 2)
+    far = lax.rem(c + 2, n)
+    far_sib = lax.rem(sib + 2, n)
+    steps = [(d, t) for t in range(n - 1) for d in (1, -1)]
+
+    def slot(d, t):
+        return t * 2 + (0 if d == 1 else 1)
+
+    def guard(d, t, sending):
+        if sending:
+            if d == 1:
+                return jnp.logical_and(r >= t, r < n - 1)
+            return jnp.logical_and(r <= n - 1 - t, r > 0)
+        if d == 1:
+            return r >= t + 1
+        return r <= n - 2 - t
+
+    def z_m(d, t):
+        b, k = r - d * t, slot(d, t)
+        return remote(mc.at[b], mc.at[b], zm_send.at[k], zm_recv.at[k], r + d, c)
+
+    def z_a(d, t):
+        b, k = r - d * t, slot(d, t)
+        return remote(ac.at[b, c], ac.at[b, c], za_send.at[k], za_recv.at[k], r + d, c)
+
+    def z_m_in(d, t):
+        b, k = r - d * (t + 1), slot(d, t)
+        return remote(mc.at[b], mc.at[b], zm_send.at[k], zm_recv.at[k], r - d, c)
+
+    def z_a_in(d, t):
+        b, k = r - d * (t + 1), slot(d, t)
+        return remote(ac.at[b, c], ac.at[b, c], za_send.at[k], za_recv.at[k], r - d, c)
+
+    def plane_a(j):
+        col, block = ((sib, c), (far, c), (sib, far))[j]
+        return remote(af.at[block], af.at[block], pa_send.at[j], pa_recv.at[j], r, col)
+
+    def plane_a_in(j):
+        block = (sib, far, far_sib)[j]
+        return remote(af.at[block], af.at[block], pa_send.at[j], pa_recv.at[j], r, sib)
+
+    def plane_c(b, k, j):
+        col, block = ((sib, c), (far, c), (sib, far))[j]
+        return remote(
+            ac.at[b, block], ac.at[b, block], pc_send.at[k, j], pc_recv.at[k, j], r, col
+        )
+
+    def plane_c_in(b, k, j):
+        block = (sib, far, far_sib)[j]
+        return remote(
+            ac.at[b, block], ac.at[b, block], pc_send.at[k, j], pc_recv.at[k, j], r, sib
+        )
+
+    def plane_m(b, k, j):
+        return remote(mc.at[b], mr.at[b], pm_send.at[k, j], pm_recv.at[k], r, (sib, far)[j])
+
+    def plane_m_on(b, k):
+        return remote(mr.at[b], mr.at[b], pm_send.at[k, 0], pm_recv.at[k], r, sib)
+
+    def plane_m_in(b, k):
+        return remote(mr.at[b], mr.at[b], pm_send.at[k, 0], pm_recv.at[k], r, sib)
+
+    is_root = c == r
+    is_hop = far == r
+    own = slot(-1, n - 2) + 1
+
+    barrier = pltpu.get_barrier_semaphore()
+    for col in (sib, far):
+        pl.semaphore_signal(
+            barrier, inc=1, device_id={"row": r, "col": col}, device_id_type=pl.DeviceIdType.MESH
+        )
+    for d in (1, -1):
+
+        @pl.when(guard(d, 0, True))
+        def _(d=d):
+            pl.semaphore_signal(
+                barrier,
+                inc=1,
+                device_id={"row": r + d, "col": c},
+                device_id_type=pl.DeviceIdType.MESH,
+            )
+
+    half = f_ref.shape[1] // RB_DEV
+    for s in range(SUPERS):
+        first = pat[s, RB_DEV * r] > 0
+        second = pat[s, RB_DEV * r + 1] > 0
+        lower = f_ref[s, :half, :]
+        mc[r, s] = jnp.where(
+            second, f_ref[s, half:, :], jnp.where(first, lower, jnp.zeros_like(lower))
+        )
+        rows = jnp.where(second, a_ref[half:, :], a_ref[:half, :])
+        ac[r, c, s] = jnp.where(pat[s, RB_DEV * c + 1] > 0, rows[:, half:], rows[:, :half])
+    af[c] = a_ref[...]
+
+    pl.semaphore_wait(barrier, 2 + (r > 0).astype(jnp.int32) + (r < n - 1).astype(jnp.int32))
+
+    for copy_of in (z_m, z_a):
+        for d in (1, -1):
+
+            @pl.when(guard(d, 0, True))
+            def _(d=d, copy_of=copy_of):
+                copy_of(d, 0).start()
+
+    plane_a(1).start()
+    plane_a(0).start()
+
+    @pl.when(is_root)
+    def _():
+        plane_m(r, own, 1).start()
+        plane_m(r, own, 0).start()
+        mr[r] = mc[r]
+
+    plane_a_in(1).wait_recv()
+    plane_a(2).start()
+
+    @pl.when(is_hop)
+    def _():
+        plane_m_in(r, own).wait_recv()
+        plane_m_on(r, own).start()
+
+    def relay(d, t):
+        b, k = r - d * (t + 1), slot(d, t)
+
+        @pl.when(guard(d, t, False))
+        def _():
+            plane_c_in(b, k, 1).wait_recv()
+            plane_c(b, k, 2).start()
+
+            @pl.when(is_hop)
+            def _():
+                plane_m_in(b, k).wait_recv()
+                plane_m_on(b, k).start()
+
+    for t in range(n - 1):
+        for d in (1, -1):
+            b, k = r - d * (t + 1), slot(d, t)
+
+            @pl.when(guard(d, t, False))
+            def _(d=d, t=t, b=b, k=k):
+                z_m_in(d, t).wait_recv()
+                if t + 1 < n - 1:
+
+                    @pl.when(guard(d, t + 1, True))
+                    def _():
+                        z_m(d, t + 1).start()
+
+                @pl.when(is_root)
+                def _():
+                    plane_m(b, k, 1).start()
+                    plane_m(b, k, 0).start()
+
+                z_a_in(d, t).wait_recv()
+                if t + 1 < n - 1:
+
+                    @pl.when(guard(d, t + 1, True))
+                    def _():
+                        z_a(d, t + 1).start()
+
+                plane_c(b, k, 1).start()
+                plane_c(b, k, 0).start()
+
+        if t > 0:
+            for d in (1, -1):
+                relay(d, t - 1)
+    for d in (1, -1):
+        relay(d, n - 2)
+
+    plane_a_in(0).wait_recv()
+    plane_a_in(2).wait_recv()
+    width = mc.shape[3]
+    depth = n * half
+    for s in range(SUPERS):
+        columns = mc[:, s].reshape(depth, width)
+        left = jnp.concatenate(
+            [
+                jnp.where(pat[s, RB_DEV * g + 1] > 0, af[g, :, half:], af[g, :, :half])
+                for g in range(n)
+            ],
+            axis=1,
+        )
+        x = jnp.dot(left, columns, preferred_element_type=jnp.float32)
+        kc_ref[s] = (-x).T.astype(jnp.bfloat16)
+        y[r, s] = jnp.where(pat[s, RB_DEV * r + 1] > 0, x[half:], x[:half]).astype(jnp.bfloat16)
+
+    for d, t in steps:
+        b, k = r - d * (t + 1), slot(d, t)
+
+        @pl.when(guard(d, t, False))
+        def _(b=b, k=k):
+            plane_c_in(b, k, 0).wait_recv()
+            plane_c_in(b, k, 2).wait_recv()
+
+    for off in range(1, n):
+        b = lax.rem(r + off, n)
+        for s in range(SUPERS):
+            left = jnp.concatenate([ac[b, g, s] for g in range(n)], axis=1)
+            y[b, s] = jnp.dot(
+                left, mc[:, s].reshape(depth, width), preferred_element_type=jnp.float32
+            ).astype(jnp.bfloat16)
+
+    @pl.when(is_root)
+    def _():
+        for off in range(1, n):
+            b = lax.rem(r + off, n)
+            mr[b] = mc[b]
+
+    is_leaf = jnp.logical_and(jnp.logical_not(is_root), jnp.logical_not(is_hop))
+
+    @pl.when(is_leaf)
+    def _():
+        plane_m_in(r, own).wait_recv()
+
+    for d, t in steps:
+        b, k = r - d * (t + 1), slot(d, t)
+
+        @pl.when(jnp.logical_and(is_leaf, guard(d, t, False)))
+        def _(b=b, k=k):
+            plane_m_in(b, k).wait_recv()
+
+    for s in range(SUPERS):
+        kk_ref[s] = p_ref[s] + lax.dot_general(
+            mr[:, s].reshape(depth, width),
+            y[:, s].reshape(depth, width),
+            (((0,), (0,)), ((), ())),
+            preferred_element_type=jnp.float32,
+        )
+
+    for d, t in steps:
+
+        @pl.when(guard(d, t, True))
+        def _(d=d, t=t):
+            z_m(d, t).wait_send()
+            z_a(d, t).wait_send()
+
+        @pl.when(guard(d, t, False))
+        def _(d=d, t=t):
+            b, k = r - d * (t + 1), slot(d, t)
+            for j in range(3):
+                plane_c(b, k, j).wait_send()
+
+            @pl.when(is_root)
+            def _():
+                plane_m(b, k, 0).wait_send()
+                plane_m(b, k, 1).wait_send()
+
+            @pl.when(is_hop)
+            def _():
+                plane_m_on(b, k).wait_send()
+
+    for j in range(3):
+        plane_a(j).wait_send()
+
+    @pl.when(is_root)
+    def _():
+        plane_m(r, own, 0).wait_send()
+        plane_m(r, own, 1).wait_send()
+
+    @pl.when(is_hop)
+    def _():
+        plane_m_on(r, own).wait_send()
+
+
+def body_kernel(n, ainv_cc, factor, inv_pivot, pattern):
+    rows, width = factor.shape[1], factor.shape[2]
+    half = rows // RB_DEV
+    slots = 2 * (n - 1)
+    vmem = pl.BlockSpec(memory_space=pltpu.VMEM)
+    dma = pltpu.SemaphoreType.DMA
+    return pl.pallas_call(
+        functools.partial(kernel, n),
+        out_shape=(
+            jax.ShapeDtypeStruct((SUPERS, width, rows), jnp.bfloat16),
+            jax.ShapeDtypeStruct(inv_pivot.shape, jnp.float32),
+        ),
+        in_specs=[pl.BlockSpec(memory_space=pltpu.SMEM), vmem, vmem, vmem],
+        out_specs=(vmem, vmem),
+        scratch_shapes=[
+            pltpu.VMEM((n, SUPERS, half, width), jnp.bfloat16),
+            pltpu.VMEM((n, SUPERS, half, width), jnp.bfloat16),
+            pltpu.VMEM((n,) + ainv_cc.shape, jnp.bfloat16),
+            pltpu.VMEM((n, n, SUPERS, half, half), jnp.bfloat16),
+            pltpu.VMEM((n, SUPERS, half, width), jnp.bfloat16),
+            dma((slots,)), dma((slots,)), dma((slots,)), dma((slots,)),
+            dma((3,)), dma((3,)),
+            dma((slots, 3)), dma((slots, 3)),
+            dma((slots + 1, 2)), dma((slots + 1,)),
+        ],
+        compiler_params=pltpu.CompilerParams(
+            collective_id=0, has_side_effects=True, vmem_limit_bytes=32 << 20
+        ),
+        cost_estimate=pl.CostEstimate(
+            flops=2 * SUPERS * 3 * width * rows * n * half,
+            bytes_accessed=8 * rows * width * SUPERS,
+            transcendentals=0,
+        ),
+    )(pattern, factor, ainv_cc, inv_pivot)
+
+
 def solution(mesh):
     placed = (P(("pole", "row"), "col"), P("pole", "row", "col"), P("pole", "row", "col"), P())
+    rows, cols = mesh.shape["row"], mesh.shape["col"]
+    fits = rows == cols and cols == 4
     return jax.shard_map(
-        body,
+        functools.partial(body_kernel, cols) if fits else body,
         mesh=mesh,
         in_specs=placed,
         out_specs=(P("pole", "col", "row"), P("pole", "row", "col")),

time: 188 us -> 31.8 us (0.17); the launches traced: 185 us -> 31.6 us
  waiting for transfers between devices: 155 us -> 0 us
  Pallas kernels: 0 us -> 25.9 us
  between operations: 14.2 us -> 0.65 us
  matrix products: 7.57 us -> 0 us
  other arithmetic: 5.21 us -> 0 us
  local copies, waits for them, and re-layouts: 2.6 us -> 5.06 us
    reduce_scatter x4 -> x0, waiting for transfers between devices: 82.3 us -> none  [the longest x2 42.1 us: body(): lax.psum_scatter(column_term(jnp.int32(0), lax.axis_size('col') * width_p...]
    psum x1 -> x0, waiting for transfers between devices: 51.7 us -> none  [spread(): return lax.psum(jnp.where(mine, x, jnp.zeros_like(x)), axis)]
    pallas_call x0 -> x1, Pallas kernels: none -> 25.9 us  [body_kernel(): pl.pallas_call(functools.partial(kernel, n), out_shape=(jax.ShapeDtypeStr...]
    all_gather x1 -> x0, waiting for transfers between devices: 20.1 us -> none  [body(): full_width = lax.all_gather(factor, 'col', axis=2, tiled=True)]
    dot_general x4 -> x0, matrix products: 7.57 us -> none  [the longest x2 4.12 us: diagonal_term(): lax.dot_general(factor_rows, cross_block, (((0,), (1,)), ((), ())), prefe...]
    another operation x5 -> x0, other arithmetic: 2.62 us -> none  [body(): return (jnp.stack(cross_list), jnp.stack(diag_list))]
    unnamed x16 -> x10, local copies, waits for them, and re-layouts: 2.53 us -> 5.06 us
    select_n x2 -> x0, other arithmetic: 2.51 us -> none  [the longest x1 2.37 us: spread(): return lax.psum(jnp.where(mine, x, jnp.zeros_like(x)), axis)]
  transfers between devices with their start and end apart: 6 -> 0, of which waited for: 6 -> 0; matrix products, arithmetic and copies ran while one was open for 3% -> 0% of each run, Pallas kernels for 0% -> 0%
where the time goes in v1:
time: 31.8 us; the launch traced here: 31.6 us
  Pallas kernels  25.9 us (81%)
  local copies, waits for them, and re-layouts  5.06 us (16%)
  between operations  0.65 us (2%)
    pallas_call x1, Pallas kernels, body_kernel(): pl.pallas_call(functools.partial(kernel, n), out_shape=(jax.ShapeDtypeStr...  25.9 us
    unnamed x10, local copies, waits for them, and re-layouts  5.06 us

profile of v1, /device:TPU:1, one launch (start us, length us, event | category | flops | bytes accessed | tf_op | source)
XLA Modules:
  0.0 31.6 jit_solution(3095555348774949796)
XLA Ops:
  0.6 0.0 copy-start
  0.6 1.0 %copy-done = f32[2,256,256]{2,1,0:T(8,128)S(1)} copy-done((f32[2,256,256]{2,1,0:T(8,128)S(1)}, f32[2,256,256]{2,1,0:T(8,128)}, u32[]{:S(2)}) %copy-start) | copy-done | bytes 524312
  1.7 0.0 copy-start.1
  1.7 0.9 %copy-done.1 = bf16[2,256,256]{2,1,0:T(8,128)(2,1)S(1)} copy-done((bf16[2,256,256]{2,1,0:T(8,128)(2,1)S(1)}, bf16[2,256,256]{2,1,0:T(8,128)(2,1)}, u32[]{:S(2)}) %copy-start.1) | copy-done | bytes 262168
  2.6 0.0 copy-start.2
  2.6 0.9 %copy-done.2 = bf16[256,256]{1,0:T(8,128)(2,1)S(1)} copy-done((bf16[256,256]{1,0:T(8,128)(2,1)S(1)}, bf16[256,256]{1,0:T(8,128)(2,1)}, u32[]{:S(2)}) %copy-start.2) | copy-done | bytes 131096
  3.5 0.0 copy-start.3
  3.5 0.7 %copy-done.3 = s32[2,8]{1,0:T(2,128)S(1)} copy-done((s32[2,8]{1,0:T(2,128)S(1)}, s32[2,8]{1,0:T(2,128)}, u32[]{:S(2)}) %copy-start.3) | copy-done | bytes 88
  4.2 25.9 %shard_map.59 = (bf16[2,256,256]{2,1,0:T(8,128)(2,1)S(1)}, f32[2,256,256]{2,1,0:T(8,128)S(1)}) custom-call(s32[2,8]{1,0:T(2,128)S(1)} %copy-done.3, bf16[2,256,256]{2,1,0:T(8,128)(2,1)S(1)} %copy-done.1, bf16[256,256]{1,0:T(8,128)(2,1)S(1)} %copy-done.2, f32[2,256,256]{2,1,0:T(8,128)S(1)} %copy-done), custom_call_target="tpu_custom_call" | custom-call | flops 402653184 | bytes 1048576 | tf_op jit(solution)/shard_map/pallas_call | solution.py:364
  30.1 0.7 %copy.8 = bf16[2,256,256]{2,1,0:T(8,128)(2,1)} copy(bf16[2,256,256]{2,1,0:T(8,128)(2,1)S(1)} %get-tuple-element.4) | data formatting | bytes 524288
  30.8 0.8 %copy.9 = f32[2,256,256]{2,1,0:T(8,128)} copy(f32[2,256,256]{2,1,0:T(8,128)S(1)} %get-tuple-element.5) | data formatting | bytes 1048576
Async XLA Ops:
  0.6 1.0 %copy-start = (f32[2,256,256]{2,1,0:T(8,128)S(1)}, f32[2,256,256]{2,1,0:T(8,128)}, u32[]{:S(2)}) copy-start(f32[2,256,256]{2,1,0:T(8,128)} %p_ref.1) | copy-start | bytes 1572868
  1.7 0.9 %copy-start.1 = (bf16[2,256,256]{2,1,0:T(8,128)(2,1)S(1)}, bf16[2,256,256]{2,1,0:T(8,128)(2,1)}, u32[]{:S(2)}) copy-start(bf16[2,256,256]{2,1,0:T(8,128)(2,1)} %f_ref.1) | copy-start | bytes 786436
  2.6 0.9 %copy-start.2 = (bf16[256,256]{1,0:T(8,128)(2,1)S(1)}, bf16[256,256]{1,0:T(8,128)(2,1)}, u32[]{:S(2)}) copy-start(bf16[256,256]{1,0:T(8,128)(2,1)} %a_ref.1) | copy-start | bytes 393220
  3.5 0.7 %copy-start.3 = (s32[2,8]{1,0:T(2,128)S(1)}, s32[2,8]{1,0:T(2,128)}, u32[]{:S(2)}) copy-start(s32[2,8]{1,0:T(2,128)} %pat.1) | copy-start | bytes 196

commit v2 on v1

--- a/solution.py
+++ b/solution.py
@@ -87,8 +87,8 @@
 
 
 def kernel(
-    n, pat, f_ref, a_ref, p_ref, kc_ref, kk_ref,
-    mc, mr, af, ac, y,
+    n, pat_hbm, f_hbm, a_hbm, p_hbm, kc_ref, kk_ref,
+    pat, f_ref, a_ref, mc, mr, af, ac, y, load_sem,
     zm_send, zm_recv, za_send, za_recv, pa_send, pa_recv, pc_send, pc_recv, pm_send, pm_recv,
 ):
     r = lax.axis_index("row")
@@ -110,17 +110,17 @@
             return r >= t + 1
         return r <= n - 2 - t
 
-    def z_m(d, t):
+    def z_m(d, t, s):
         b, k = r - d * t, slot(d, t)
-        return remote(mc.at[b], mc.at[b], zm_send.at[k], zm_recv.at[k], r + d, c)
+        return remote(mc.at[b, s], mc.at[b, s], zm_send.at[k, s], zm_recv.at[k, s], r + d, c)
 
     def z_a(d, t):
         b, k = r - d * t, slot(d, t)
         return remote(ac.at[b, c], ac.at[b, c], za_send.at[k], za_recv.at[k], r + d, c)
 
-    def z_m_in(d, t):
+    def z_m_in(d, t, s):
         b, k = r - d * (t + 1), slot(d, t)
-        return remote(mc.at[b], mc.at[b], zm_send.at[k], zm_recv.at[k], r - d, c)
+        return remote(mc.at[b, s], mc.at[b, s], zm_send.at[k, s], zm_recv.at[k, s], r - d, c)
 
     def z_a_in(d, t):
         b, k = r - d * (t + 1), slot(d, t)
@@ -146,18 +146,28 @@
             ac.at[b, block], ac.at[b, block], pc_send.at[k, j], pc_recv.at[k, j], r, sib
         )
 
-    def plane_m(b, k, j):
-        return remote(mc.at[b], mr.at[b], pm_send.at[k, j], pm_recv.at[k], r, (sib, far)[j])
-
-    def plane_m_on(b, k):
-        return remote(mr.at[b], mr.at[b], pm_send.at[k, 0], pm_recv.at[k], r, sib)
-
-    def plane_m_in(b, k):
-        return remote(mr.at[b], mr.at[b], pm_send.at[k, 0], pm_recv.at[k], r, sib)
+    def plane_m(b, k, s, j):
+        return remote(
+            mc.at[b, s], mr.at[b, s], pm_send.at[k, s, j], pm_recv.at[k, s], r, (sib, far)[j]
+        )
+
+    def plane_m_on(b, k, s):
+        return remote(mr.at[b, s], mr.at[b, s], pm_send.at[k, s, 0], pm_recv.at[k, s], r, sib)
+
+    plane_m_in = plane_m_on
 
     is_root = c == r
     is_hop = far == r
     own = slot(-1, n - 2) + 1
+
+    loads = [
+        pltpu.make_async_copy(src, dst, load_sem.at[i])
+        for i, (src, dst) in enumerate(
+            ((pat_hbm, pat), (f_hbm, f_ref), (a_hbm, a_ref), (p_hbm, kk_ref))
+        )
+    ]
+    for load in loads:
+        load.start()
 
     barrier = pltpu.get_barrier_semaphore()
     for col in (sib, far):
@@ -176,6 +186,8 @@
             )
 
     half = f_ref.shape[1] // RB_DEV
+    for load in loads[:3]:
+        load.wait()
     for s in range(SUPERS):
         first = pat[s, RB_DEV * r] > 0
         second = pat[s, RB_DEV * r + 1] > 0
@@ -189,61 +201,67 @@
 
     pl.semaphore_wait(barrier, 2 + (r > 0).astype(jnp.int32) + (r < n - 1).astype(jnp.int32))
 
-    for copy_of in (z_m, z_a):
+    for s in range(SUPERS):
         for d in (1, -1):
 
             @pl.when(guard(d, 0, True))
-            def _(d=d, copy_of=copy_of):
-                copy_of(d, 0).start()
+            def _(d=d, s=s):
+                z_m(d, 0, s).start()
+
+    for d in (1, -1):
+
+        @pl.when(guard(d, 0, True))
+        def _(d=d):
+            z_a(d, 0).start()
 
     plane_a(1).start()
     plane_a(0).start()
 
     @pl.when(is_root)
     def _():
-        plane_m(r, own, 1).start()
-        plane_m(r, own, 0).start()
+        for s in range(SUPERS):
+            plane_m(r, own, s, 1).start()
+            plane_m(r, own, s, 0).start()
         mr[r] = mc[r]
-
-    plane_a_in(1).wait_recv()
-    plane_a(2).start()
-
-    @pl.when(is_hop)
-    def _():
-        plane_m_in(r, own).wait_recv()
-        plane_m_on(r, own).start()
 
     def relay(d, t):
         b, k = r - d * (t + 1), slot(d, t)
 
         @pl.when(guard(d, t, False))
         def _():
+            @pl.when(is_hop)
+            def _():
+                for s in range(SUPERS):
+                    plane_m_in(b, k, s).wait_recv()
+                    plane_m_on(b, k, s).start()
+
             plane_c_in(b, k, 1).wait_recv()
             plane_c(b, k, 2).start()
 
-            @pl.when(is_hop)
-            def _():
-                plane_m_in(b, k).wait_recv()
-                plane_m_on(b, k).start()
-
     for t in range(n - 1):
+        for s in range(SUPERS):
+            for d in (1, -1):
+                b, k = r - d * (t + 1), slot(d, t)
+
+                @pl.when(guard(d, t, False))
+                def _(d=d, t=t, b=b, k=k, s=s):
+                    z_m_in(d, t, s).wait_recv()
+                    if t + 1 < n - 1:
+
+                        @pl.when(guard(d, t + 1, True))
+                        def _():
+                            z_m(d, t + 1, s).start()
+
+                    @pl.when(is_root)
+                    def _():
+                        plane_m(b, k, s, 1).start()
+                        plane_m(b, k, s, 0).start()
+
         for d in (1, -1):
             b, k = r - d * (t + 1), slot(d, t)
 
             @pl.when(guard(d, t, False))
             def _(d=d, t=t, b=b, k=k):
-                z_m_in(d, t).wait_recv()
-                if t + 1 < n - 1:
-
-                    @pl.when(guard(d, t + 1, True))
-                    def _():
-                        z_m(d, t + 1).start()
-
-                @pl.when(is_root)
-                def _():
-                    plane_m(b, k, 1).start()
-                    plane_m(b, k, 0).start()
-
                 z_a_in(d, t).wait_recv()
                 if t + 1 < n - 1:
 
@@ -254,7 +272,17 @@
                 plane_c(b, k, 1).start()
                 plane_c(b, k, 0).start()
 
-        if t > 0:
+        if t == 0:
+            plane_a_in(1).wait_recv()
+            plane_a(2).start()
+
+            @pl.when(is_hop)
+            def _():
+                for s in range(SUPERS):
+                    plane_m_in(r, own, s).wait_recv()
+                    plane_m_on(r, own, s).start()
+
+        else:
             for d in (1, -1):
                 relay(d, t - 1)
     for d in (1, -1):
@@ -303,17 +331,20 @@
 
     @pl.when(is_leaf)
     def _():
-        plane_m_in(r, own).wait_recv()
+        for s in range(SUPERS):
+            plane_m_in(r, own, s).wait_recv()
 
     for d, t in steps:
         b, k = r - d * (t + 1), slot(d, t)
 
         @pl.when(jnp.logical_and(is_leaf, guard(d, t, False)))
         def _(b=b, k=k):
-            plane_m_in(b, k).wait_recv()
-
+            for s in range(SUPERS):
+                plane_m_in(b, k, s).wait_recv()
+
+    loads[3].wait()
     for s in range(SUPERS):
-        kk_ref[s] = p_ref[s] + lax.dot_general(
+        kk_ref[s] = kk_ref[s] + lax.dot_general(
             mr[:, s].reshape(depth, width),
             y[:, s].reshape(depth, width),
             (((0,), (0,)), ((), ())),
@@ -324,7 +355,8 @@
 
         @pl.when(guard(d, t, True))
         def _(d=d, t=t):
-            z_m(d, t).wait_send()
+            for s in range(SUPERS):
+                z_m(d, t, s).wait_send()
             z_a(d, t).wait_send()
 
         @pl.when(guard(d, t, False))
@@ -335,24 +367,28 @@
 
             @pl.when(is_root)
             def _():
-                plane_m(b, k, 0).wait_send()
-                plane_m(b, k, 1).wait_send()
+                for s in range(SUPERS):
+                    plane_m(b, k, s, 0).wait_send()
+                    plane_m(b, k, s, 1).wait_send()
 
             @pl.when(is_hop)
             def _():
-                plane_m_on(b, k).wait_send()
+                for s in range(SUPERS):
+                    plane_m_on(b, k, s).wait_send()
 
     for j in range(3):
         plane_a(j).wait_send()
 
     @pl.when(is_root)
     def _():
-        plane_m(r, own, 0).wait_send()
-        plane_m(r, own, 1).wait_send()
+        for s in range(SUPERS):
+            plane_m(r, own, s, 0).wait_send()
+            plane_m(r, own, s, 1).wait_send()
 
     @pl.when(is_hop)
     def _():
-        plane_m_on(r, own).wait_send()
+        for s in range(SUPERS):
+            plane_m_on(r, own, s).wait_send()
 
 
 def body_kernel(n, ainv_cc, factor, inv_pivot, pattern):
@@ -367,18 +403,22 @@
             jax.ShapeDtypeStruct((SUPERS, width, rows), jnp.bfloat16),
             jax.ShapeDtypeStruct(inv_pivot.shape, jnp.float32),
         ),
-        in_specs=[pl.BlockSpec(memory_space=pltpu.SMEM), vmem, vmem, vmem],
+        in_specs=[pl.BlockSpec(memory_space=pltpu.MemorySpace.HBM)] * 4,
         out_specs=(vmem, vmem),
         scratch_shapes=[
+            pltpu.SMEM(pattern.shape, jnp.int32),
+            pltpu.VMEM(factor.shape, jnp.bfloat16),
+            pltpu.VMEM(ainv_cc.shape, jnp.bfloat16),
             pltpu.VMEM((n, SUPERS, half, width), jnp.bfloat16),
             pltpu.VMEM((n, SUPERS, half, width), jnp.bfloat16),
             pltpu.VMEM((n,) + ainv_cc.shape, jnp.bfloat16),
             pltpu.VMEM((n, n, SUPERS, half, half), jnp.bfloat16),
             pltpu.VMEM((n, SUPERS, half, width), jnp.bfloat16),
-            dma((slots,)), dma((slots,)), dma((slots,)), dma((slots,)),
+            dma((4,)),
+            dma((slots, SUPERS)), dma((slots, SUPERS)), dma((slots,)), dma((slots,)),
             dma((3,)), dma((3,)),
             dma((slots, 3)), dma((slots, 3)),
-            dma((slots + 1, 2)), dma((slots + 1,)),
+            dma((slots + 1, SUPERS, 2)), dma((slots + 1, SUPERS)),
         ],
         compiler_params=pltpu.CompilerParams(
             collective_id=0, has_side_effects=True, vmem_limit_bytes=32 << 20
@@ -388,7 +428,12 @@
             bytes_accessed=8 * rows * width * SUPERS,
             transcendentals=0,
         ),
-    )(pattern, factor, ainv_cc, inv_pivot)
+    )(
+        *(
+            pltpu.with_memory_space_constraint(x, pltpu.MemorySpace.HBM)
+            for x in (pattern, factor, ainv_cc, inv_pivot)
+        )
+    )
 
 
 def solution(mesh):

time: 31.8 us -> 26.5 us (0.83)
  local copies, waits for them, and re-layouts: 5.06 us -> 1.5 us
  Pallas kernels: 25.9 us -> 24.2 us
    unnamed x10 -> x2, local copies, waits for them, and re-layouts: 5.06 us -> 1.5 us
    pallas_call x1, Pallas kernels: 25.9 us -> 24.2 us  [body_kernel(): pl.pallas_call(functools.partial(kernel, n), out_shape=(jax.ShapeDtypeStr...]
where the time goes in v2:
time: 26.5 us; the launch traced here: 26.4 us
  Pallas kernels  24.2 us (91%)
  local copies, waits for them, and re-layouts  1.5 us (6%)
  between operations  0.64 us (2%)
    pallas_call x1, Pallas kernels, body_kernel(): pl.pallas_call(functools.partial(kernel, n), out_shape=(jax.ShapeDtypeStr...  24.2 us
    unnamed x2, local copies, waits for them, and re-layouts  1.5 us

profile of v2, /device:TPU:1, one launch (start us, length us, event | category | flops | bytes accessed | tf_op | source)
XLA Modules:
  0.0 26.4 jit_solution(14183323595020045510)
XLA Ops:
  0.6 24.2 %shard_map.59 = (bf16[2,256,256]{2,1,0:T(8,128)(2,1)S(1)}, f32[2,256,256]{2,1,0:T(8,128)S(1)}) custom-call(s32[2,8]{1,0:T(2,128)} %pat_hbm.1, bf16[2,256,256]{2,1,0:T(8,128)(2,1)} %f_hbm.1, bf16[256,256]{1,0:T(8,128)(2,1)} %a_hbm.1, f32[2,256,256]{2,1,0:T(8,128)} %p_hbm.1), custom_call_target="tpu_custom_call" | custom-call | flops 402653184 | bytes 1048576 | tf_op jit(solution)/shard_map/pallas_call | solution.py:400
  24.9 0.7 %copy.8 = bf16[2,256,256]{2,1,0:T(8,128)(2,1)} copy(bf16[2,256,256]{2,1,0:T(8,128)(2,1)S(1)} %get-tuple-element.4) | data formatting | bytes 524288
  25.6 0.8 %copy.9 = f32[2,256,256]{2,1,0:T(8,128)} copy(f32[2,256,256]{2,1,0:T(8,128)S(1)} %get-tuple-element.5) | data formatting | bytes 1048576

commit v3 on v2

--- a/solution.py
+++ b/solution.py
@@ -186,33 +186,34 @@
             )
 
     half = f_ref.shape[1] // RB_DEV
-    for load in loads[:3]:
-        load.wait()
+    loads[0].wait()
+    loads[1].wait()
     for s in range(SUPERS):
-        first = pat[s, RB_DEV * r] > 0
-        second = pat[s, RB_DEV * r + 1] > 0
         lower = f_ref[s, :half, :]
         mc[r, s] = jnp.where(
-            second, f_ref[s, half:, :], jnp.where(first, lower, jnp.zeros_like(lower))
-        )
-        rows = jnp.where(second, a_ref[half:, :], a_ref[:half, :])
+            pat[s, RB_DEV * r + 1] > 0,
+            f_ref[s, half:, :],
+            jnp.where(pat[s, RB_DEV * r] > 0, lower, jnp.zeros_like(lower)),
+        )
+    loads[2].wait()
+    for s in range(SUPERS):
+        rows = jnp.where(pat[s, RB_DEV * r + 1] > 0, a_ref[half:, :], a_ref[:half, :])
         ac[r, c, s] = jnp.where(pat[s, RB_DEV * c + 1] > 0, rows[:, half:], rows[:, :half])
     af[c] = a_ref[...]
 
     pl.semaphore_wait(barrier, 2 + (r > 0).astype(jnp.int32) + (r < n - 1).astype(jnp.int32))
 
-    for s in range(SUPERS):
+    items = ("a", 0, 1)
+
+    def send(item, d, t):
+        (z_a(d, t) if item == "a" else z_m(d, t, item)).start()
+
+    for item in items:
         for d in (1, -1):
 
             @pl.when(guard(d, 0, True))
-            def _(d=d, s=s):
-                z_m(d, 0, s).start()
-
-    for d in (1, -1):
-
-        @pl.when(guard(d, 0, True))
-        def _(d=d):
-            z_a(d, 0).start()
+            def _(d=d, item=item):
+                send(item, d, 0)
 
     plane_a(1).start()
     plane_a(0).start()
@@ -224,69 +225,70 @@
             plane_m(r, own, s, 0).start()
         mr[r] = mc[r]
 
-    def relay(d, t):
+    def arrive(item, d, t):
         b, k = r - d * (t + 1), slot(d, t)
 
         @pl.when(guard(d, t, False))
         def _():
-            @pl.when(is_hop)
-            def _():
-                for s in range(SUPERS):
-                    plane_m_in(b, k, s).wait_recv()
-                    plane_m_on(b, k, s).start()
-
-            plane_c_in(b, k, 1).wait_recv()
-            plane_c(b, k, 2).start()
-
-    for t in range(n - 1):
-        for s in range(SUPERS):
-            for d in (1, -1):
-                b, k = r - d * (t + 1), slot(d, t)
-
-                @pl.when(guard(d, t, False))
-                def _(d=d, t=t, b=b, k=k, s=s):
-                    z_m_in(d, t, s).wait_recv()
-                    if t + 1 < n - 1:
-
-                        @pl.when(guard(d, t + 1, True))
-                        def _():
-                            z_m(d, t + 1, s).start()
-
-                    @pl.when(is_root)
-                    def _():
-                        plane_m(b, k, s, 1).start()
-                        plane_m(b, k, s, 0).start()
-
-        for d in (1, -1):
-            b, k = r - d * (t + 1), slot(d, t)
-
-            @pl.when(guard(d, t, False))
-            def _(d=d, t=t, b=b, k=k):
-                z_a_in(d, t).wait_recv()
-                if t + 1 < n - 1:
-
-                    @pl.when(guard(d, t + 1, True))
-                    def _():
-                        z_a(d, t + 1).start()
-
+            (z_a_in(d, t) if item == "a" else z_m_in(d, t, item)).wait_recv()
+            if t + 1 < n - 1:
+
+                @pl.when(guard(d, t + 1, True))
+                def _():
+                    send(item, d, t + 1)
+
+            if item == "a":
                 plane_c(b, k, 1).start()
                 plane_c(b, k, 0).start()
-
-        if t == 0:
-            plane_a_in(1).wait_recv()
-            plane_a(2).start()
-
-            @pl.when(is_hop)
+            else:
+
+                @pl.when(is_root)
+                def _():
+                    plane_m(b, k, item, 1).start()
+                    plane_m(b, k, item, 0).start()
+
+    def relay(item, d, t):
+        b, k = r - d * (t + 1), slot(d, t)
+        if item == "a":
+
+            @pl.when(guard(d, t, False))
             def _():
-                for s in range(SUPERS):
-                    plane_m_in(r, own, s).wait_recv()
-                    plane_m_on(r, own, s).start()
+                plane_c_in(b, k, 1).wait_recv()
+                plane_c(b, k, 2).start()
 
         else:
-            for d in (1, -1):
-                relay(d, t - 1)
-    for d in (1, -1):
-        relay(d, n - 2)
+
+            @pl.when(jnp.logical_and(is_hop, guard(d, t, False)))
+            def _():
+                plane_m_in(b, k, item).wait_recv()
+                plane_m_on(b, k, item).start()
+
+    def relay_own():
+        plane_a_in(1).wait_recv()
+        plane_a(2).start()
+
+        @pl.when(is_hop)
+        def _():
+            for s in range(SUPERS):
+                plane_m_in(r, own, s).wait_recv()
+                plane_m_on(r, own, s).start()
+
+    events = [(item, t) for t in range(n - 1) for item in items]
+    waiting = [None]
+    for item, t in events:
+        for d in (1, -1):
+            arrive(item, d, t)
+        waiting.append((item, t))
+        if len(waiting) > 2:
+            late = waiting.pop(0)
+            if late is None:
+                relay_own()
+            else:
+                for d in (1, -1):
+                    relay(late[0], d, late[1])
+    for late in waiting:
+        for d in (1, -1):
+            relay(late[0], d, late[1])
 
     plane_a_in(0).wait_recv()
     plane_a_in(2).wait_recv()
@@ -391,13 +393,24 @@
             plane_m_on(r, own, s).wait_send()
 
 
+def write_out(cross_ref, diag_ref, cross_out, diag_out, sem):
+    copies = [
+        pltpu.make_async_copy(diag_ref, diag_out, sem.at[0]),
+        pltpu.make_async_copy(cross_ref, cross_out, sem.at[1]),
+    ]
+    for copy in copies:
+        copy.start()
+    for copy in copies:
+        copy.wait()
+
+
 def body_kernel(n, ainv_cc, factor, inv_pivot, pattern):
     rows, width = factor.shape[1], factor.shape[2]
     half = rows // RB_DEV
     slots = 2 * (n - 1)
     vmem = pl.BlockSpec(memory_space=pltpu.VMEM)
     dma = pltpu.SemaphoreType.DMA
-    return pl.pallas_call(
+    cross, diag = pl.pallas_call(
         functools.partial(kernel, n),
         out_shape=(
             jax.ShapeDtypeStruct((SUPERS, width, rows), jnp.bfloat16),
@@ -436,6 +449,18 @@
     )
 
 
+    return pl.pallas_call(
+        write_out,
+        out_shape=(
+            jax.ShapeDtypeStruct(cross.shape, cross.dtype),
+            jax.ShapeDtypeStruct(diag.shape, diag.dtype),
+        ),
+        in_specs=[vmem, vmem],
+        out_specs=(pl.BlockSpec(memory_space=pl.ANY), pl.BlockSpec(memory_space=pl.ANY)),
+        scratch_shapes=[dma((2,))],
+    )(*(pltpu.with_memory_space_constraint(x, pltpu.MemorySpace.VMEM) for x in (cross, diag)))
+
+
 def solution(mesh):
     placed = (P(("pole", "row"), "col"), P("pole", "row", "col"), P("pole", "row", "col"), P())
     rows, cols = mesh.shape["row"], mesh.shape["col"]

time: 26.5 us -> 24.5 us (0.925)
  local copies, waits for them, and re-layouts: 1.5 us -> 0 us
  Pallas kernels: 24.2 us -> 23.7 us
    unnamed x2 -> x0, local copies, waits for them, and re-layouts: 1.5 us -> none
    pallas_call x1, Pallas kernels: 24.2 us -> 22.8 us  [body_kernel(): pl.pallas_call(functools.partial(kernel, n), out_shape=(jax.ShapeDtypeStr...]
    pallas_call x0 -> x1, Pallas kernels: none -> 0.89 us  [body_kernel(): pl.pallas_call(write_out, out_shape=(jax.ShapeDtypeStruct(cross.shape, cr...]
where the time goes in v3:
time: 24.5 us; the launch traced here: 24.3 us
  Pallas kernels  23.7 us (97%)
  between operations  0.64 us (3%)
    pallas_call x1, Pallas kernels, body_kernel(): pl.pallas_call(functools.partial(kernel, n), out_shape=(jax.ShapeDtypeStr...  22.8 us
    pallas_call x1, Pallas kernels, body_kernel(): pl.pallas_call(write_out, out_shape=(jax.ShapeDtypeStruct(cross.shape, cr...  0.89 us

profile of v3, /device:TPU:1, one launch (start us, length us, event | category | flops | bytes accessed | tf_op | source)
XLA Modules:
  0.0 24.3 jit_solution(14996312546809622655)
XLA Ops:
  0.6 22.8 %shard_map.59 = (bf16[2,256,256]{2,1,0:T(8,128)(2,1)S(1)}, f32[2,256,256]{2,1,0:T(8,128)S(1)}) custom-call(s32[2,8]{1,0:T(2,128)} %pat_hbm.1, bf16[2,256,256]{2,1,0:T(8,128)(2,1)} %f_hbm.1, bf16[256,256]{1,0:T(8,128)(2,1)} %a_hbm.1, f32[2,256,256]{2,1,0:T(8,128)} %p_hbm.1), custom_call_target="tpu_custom_call" | custom-call | flops 402653184 | bytes 1048576 | tf_op jit(solution)/shard_map/pallas_call | solution.py:413
  23.4 0.9 %shard_map.60 = (bf16[2,256,256]{2,1,0:T(8,128)(2,1)}, f32[2,256,256]{2,1,0:T(8,128)}) custom-call(bf16[2,256,256]{2,1,0:T(8,128)(2,1)S(1)} %get-tuple-element.4.cross_ref, f32[2,256,256]{2,1,0:T(8,128)S(1)} %get-tuple-element.5.diag_ref), custom_call_target="tpu_custom_call" | custom-call | tf_op jit(solution)/shard_map/pallas_call | solution.py:452

commit v4 on v3

--- a/solution.py
+++ b/solution.py
@@ -286,7 +286,7 @@
             else:
                 for d in (1, -1):
                     relay(late[0], d, late[1])
-    for late in waiting:
+    for late in waiting[:-1]:
         for d in (1, -1):
             relay(late[0], d, late[1])
 
@@ -307,6 +307,15 @@
         kc_ref[s] = (-x).T.astype(jnp.bfloat16)
         y[r, s] = jnp.where(pat[s, RB_DEV * r + 1] > 0, x[half:], x[:half]).astype(jnp.bfloat16)
 
+    for d in (1, -1):
+        relay(waiting[-1][0], d, waiting[-1][1])
+
+    @pl.when(is_root)
+    def _():
+        for off in range(1, n):
+            b = lax.rem(r + off, n)
+            mr[b] = mc[b]
+
     for d, t in steps:
         b, k = r - d * (t + 1), slot(d, t)
 
@@ -322,12 +331,6 @@
             y[b, s] = jnp.dot(
                 left, mc[:, s].reshape(depth, width), preferred_element_type=jnp.float32
             ).astype(jnp.bfloat16)
-
-    @pl.when(is_root)
-    def _():
-        for off in range(1, n):
-            b = lax.rem(r + off, n)
-            mr[b] = mc[b]
 
     is_leaf = jnp.logical_and(jnp.logical_not(is_root), jnp.logical_not(is_hop))
 

time: 24.5 us -> 24.5 us (level)
  no operation moved by 1% of the time
where the time goes in v4:
time: 24.5 us; the launch traced here: 24.3 us
  Pallas kernels  23.7 us (97%)
  between operations  0.64 us (3%)
    pallas_call x1, Pallas kernels, body_kernel(): pl.pallas_call(functools.partial(kernel, n), out_shape=(jax.ShapeDtypeStr...  22.8 us
    pallas_call x1, Pallas kernels, body_kernel(): pl.pallas_call(write_out, out_shape=(jax.ShapeDtypeStruct(cross.shape, cr...  0.89 us

profile of v4, /device:TPU:1, one launch (start us, length us, event | category | flops | bytes accessed | tf_op | source)
XLA Modules:
  0.0 24.3 jit_solution(1084181335102492044)
XLA Ops:
  0.6 22.8 %shard_map.59 = (bf16[2,256,256]{2,1,0:T(8,128)(2,1)S(1)}, f32[2,256,256]{2,1,0:T(8,128)S(1)}) custom-call(s32[2,8]{1,0:T(2,128)} %pat_hbm.1, bf16[2,256,256]{2,1,0:T(8,128)(2,1)} %f_hbm.1, bf16[256,256]{1,0:T(8,128)(2,1)} %a_hbm.1, f32[2,256,256]{2,1,0:T(8,128)} %p_hbm.1), custom_call_target="tpu_custom_call" | custom-call | flops 402653184 | bytes 1048576 | tf_op jit(solution)/shard_map/pallas_call | solution.py:416
  23.4 0.9 %shard_map.60 = (bf16[2,256,256]{2,1,0:T(8,128)(2,1)}, f32[2,256,256]{2,1,0:T(8,128)}) custom-call(bf16[2,256,256]{2,1,0:T(8,128)(2,1)S(1)} %get-tuple-element.4.cross_ref, f32[2,256,256]{2,1,0:T(8,128)S(1)} %get-tuple-element.5.diag_ref), custom_call_target="tpu_custom_call" | custom-call | tf_op jit(solution)/shard_map/pallas_call | solution.py:455
